TPU v7x, 256 devices: a whole 4x4x8 slice. The times are simulated.
256 devices in a mesh: ctx: 64 (over y, z, core), tp: 4 (over x).
Axes of the slice: x: 4, y: 4, z: 8, core: 2. Of those that a mesh axis runs over, the one named last changes fastest.
Arguments:
- first_stream: bfloat16 [32768, 8192], P(('ctx', 'tp')), may hold values from -6 to 6
- second_stream: bfloat16 [32768, 8192], P(('ctx', 'tp')), may hold values from -6 to 6
- value_stream: bfloat16 [32768, 8192], P(('ctx', 'tp')), may hold values from -6 to 6
- short_filter: bfloat16 [3, 7, 512], replicated, may hold values from -2 to 2
- long_filter: bfloat16 [128, 512], replicated, may hold values from -0.5 to 0.5
- skip_gain: float32 [8192], replicated, may hold values from -3 to 3
- lengths: int32 [16], replicated, may hold values from 1 to 4096, 32768 in all
Outputs:
- mixed: bfloat16 [8192, 32768], P(('ctx', 'tp'))
Inputs may be any that keep to these rules, and one draw needn't show every extreme that they name: The lengths of the 16 segments packed into the window in order; they sum to 32768.
All inputs are finite; a program needn't handle non-finite values.
Results may differ from a plain program's by a relative error of at most 0.0085.
Values may be sent and summed in bfloat16 or wider, within the bound.
A program may use at most 192 MiB of HBM per device.

v0:
```python
import functools

import jax
import jax.numpy as jnp
from jax import lax
from jax.experimental import pallas as pl
from jax.experimental.pallas import tpu as pltpu
from jax.sharding import PartitionSpec as P

MESH = pl.DeviceIdType.MESH
CTX = 64
TP = 4
NDEV = CTX * TP
ROWS = 128
LANES = 128
CH = 32
TILES = 64
SHORT = 7
HALO = 8
STRIDE = 43
HALO_LAG = 3
PER_CHUNK = 4
CHUNKS = TILES // PER_CHUNK
LAG = 3
F32 = jnp.float32
BF16 = jnp.bfloat16


def starts_of(lengths_ref, positions):
    begin = jnp.zeros_like(positions)
    start = jnp.int32(0)
    for j in range(15):
        start = start + lengths_ref[j]
        begin = jnp.where(positions >= start, start, begin)
    return begin


def segment_start(lengths_ref, position):
    begin = jnp.int32(0)
    start = jnp.int32(0)
    for j in range(15):
        start = start + lengths_ref[j]
        begin = jnp.where(position >= start, start, begin)
    return begin


def iota(shape, dim):
    return lax.broadcasted_iota(jnp.int32, shape, dim)


def nt_dot(a, b):
    return lax.dot_general(a, b, (((1,), (1,)), ((), ())), preferred_element_type=F32)


def kernel(
    lengths_ref, first_hbm, second_hbm, value_hbm, short_ref, long_ref, skip_ref, out_ref,
    streams, raw_halo, padded, taps, keep, long_rows, own_mask, prev_mask, head_mask,
    send_buf, recv_buf, halo_buf, out_buf, ident,
    load_sem, raw_send, raw_recv, one_send, one_recv, own_sem, halo_send, halo_recv, two_send, two_recv,
):
    ctx = lax.axis_index("ctx")
    tp = lax.axis_index("tp")
    me = ctx * TP + tp
    after = lax.rem(me + 1, NDEV)
    before = lax.rem(me + NDEV - 1, NDEV)
    after_ctx, after_tp = after // TP, lax.rem(after, TP)
    sources = (first_hbm, second_hbm, value_hbm)

    barrier = pltpu.get_barrier_semaphore()

    def greet(i, carry):
        pl.semaphore_signal(
            barrier, inc=1, device_id=(lax.rem(ctx + i, CTX), tp), device_id_type=MESH
        )
        return carry

    for d in range(1, TP):
        pl.semaphore_signal(
            barrier, inc=1, device_id=(ctx, lax.rem(tp + d, TP)), device_id_type=MESH
        )
    for other in (after, before):
        pl.semaphore_signal(
            barrier, inc=1, device_id=(other // TP, lax.rem(other, TP)), device_id_type=MESH
        )
    lax.fori_loop(1, CTX, greet, 0)

    loads = [
        pltpu.make_async_copy(sources[s], streams.at[s], load_sem.at[s]) for s in range(3)
    ]
    for load in loads:
        load.start()

    spread = (iota((LANES, 2048), 1) // 16 == iota((LANES, 2048), 0)).astype(BF16)
    for s in range(3):
        for q in range(4):
            wide = jnp.dot(
                short_ref[s, :, q * LANES : (q + 1) * LANES], spread, preferred_element_type=F32
            )
            for j in range(16):
                taps[q * 16 + j, s, 0:SHORT, :] = wide[:, j * LANES : (j + 1) * LANES]
    eye = (iota((LANES, LANES), 0) == iota((LANES, LANES), 1)).astype(BF16)
    ident[...] = eye
    for q in range(4):
        long_rows[q * LANES : (q + 1) * LANES, :] = nt_dot(
            eye, long_ref[:, q * LANES : (q + 1) * LANES]
        )
    place = me * ROWS + iota((ROWS, LANES), 0)
    offset = place - starts_of(lengths_ref, place)
    for k in range(1, SHORT):
        keep[k] = jnp.where(offset >= k, 1.0, 0.0)
    for b in range(4):
        base = ctx * 512 + b * ROWS
        at = base + iota((LANES, LANES), 1)
        begin = starts_of(lengths_ref, at)
        src = base + iota((LANES, LANES), 0)
        own_mask[b] = jnp.where((src >= begin) & (src <= at), 1.0, 0.0).astype(BF16)
        head = segment_start(lengths_ref, base)
        prev_at = base - ROWS + iota((CH, LANES), 1)
        prev_mask[b] = jnp.where(prev_at >= head, 1.0, 0.0).astype(BF16)
        row_at = base + iota((CH, LANES), 1)
        head_mask[b] = jnp.where(starts_of(lengths_ref, row_at) <= base, 1.0, 0.0)

    pl.semaphore_wait(barrier, CTX - 1 + TP - 1 + 2)

    def send_raw(k):
        def one(j, carry):
            i = k * PER_CHUNK + j
            tile = lax.rem(after_ctx + STRIDE * i, CTX)
            for s in range(3):
                pltpu.make_async_remote_copy(
                    sources[s].at[pl.ds(ROWS - HALO, HALO), pl.ds(pl.multiple_of(tile * LANES, LANES), LANES)],
                    raw_halo.at[i, s],
                    raw_send,
                    raw_recv.at[k],
                    device_id=(after_ctx, after_tp),
                    device_id_type=MESH,
                ).start()
            return carry

        lax.fori_loop(0, PER_CHUNK, one, 0)

    def short_chunk(k):
        here = raw_halo.at[pl.ds(k * PER_CHUNK, PER_CHUNK)]
        pltpu.make_async_copy(here, here, raw_recv.at[k]).wait()

        def one(j, carry):
            i = k * PER_CHUNK + j
            tile = lax.rem(ctx + STRIDE * i, CTX)
            lanes = pl.ds(pl.multiple_of(tile * LANES, LANES), LANES)
            features = []
            for s in range(3):
                padded[s, 0:HALO, :] = raw_halo[i, s].astype(F32)
                padded[s, HALO:, :] = streams[s, :, lanes].astype(F32)
            for s in range(3):
                total = padded[s, HALO:, :] * taps[tile, s, 0:1, :]
                for t in range(1, SHORT):
                    total += (padded[s, HALO - t : HALO - t + ROWS, :] * keep[t]) * taps[tile, s, t : t + 1, :]
                features.append(total)
            mixed_in = (features[0] * features[2]).astype(BF16)
            gate = features[1].astype(BF16)
            unit = ident[...]
            send_buf[i, :, 0] = nt_dot(unit, mixed_in).astype(BF16).reshape(TP, CH, LANES)
            send_buf[i, :, 1] = nt_dot(unit, gate).astype(BF16).reshape(TP, CH, LANES)
            return carry

        lax.fori_loop(0, PER_CHUNK, one, 0)
        part = pl.ds(k * PER_CHUNK, PER_CHUNK)
        for d in range(1, TP):
            to = lax.rem(tp + d, TP)
            pltpu.make_async_remote_copy(
                send_buf.at[part, to],
                recv_buf.at[tp, part],
                one_send,
                one_recv.at[k],
                device_id=(ctx, to),
                device_id_type=MESH,
            ).start()
        pltpu.make_async_copy(send_buf.at[part, tp], recv_buf.at[tp, part], own_sem.at[k]).start()

    def forward_chunk(k):
        part = pl.ds(k * PER_CHUNK, PER_CHUNK)
        three = recv_buf.at[pl.ds(0, 3), part]
        pltpu.make_async_copy(three, three, one_recv.at[k]).wait()
        one_part = recv_buf.at[0, part]
        pltpu.make_async_copy(one_part, one_part, own_sem.at[k]).wait()

        def one(j, carry):
            i = k * PER_CHUNK + j
            slot = lax.rem(i + TILES - HALO_LAG, TILES)
            pltpu.make_async_remote_copy(
                recv_buf.at[3, i, 0],
                halo_buf.at[slot],
                halo_send,
                halo_recv.at[slot],
                device_id=(lax.rem(ctx + 1, CTX), tp),
                device_id_type=MESH,
            ).start()
            return carry

        lax.fori_loop(0, PER_CHUNK, one, 0)

    lower = (iota((LANES, LANES), 0) > iota((LANES, LANES), 1)).astype(BF16)

    def circulant(row):
        base = jnp.broadcast_to(row, (8, LANES))
        sub = iota((8, LANES), 0)
        for bit in (1, 2, 4):
            base = jnp.where((sub & bit) != 0, pltpu.roll(base, bit, 1), base)
        return jnp.concatenate(
            [base] + [pltpu.roll(base, 8 * q, 1) for q in range(1, 16)], axis=0
        ).astype(BF16)

    def pick(wide):
        parts = []
        for r in range(wide.shape[0] // CH):
            parts.append(wide[r * CH : r * CH + 16, :LANES])
            parts.append(wide[r * CH + 16 : (r + 1) * CH, LANES:])
        return jnp.concatenate(parts, axis=0)

    def long_chunk(k):
        def one(j, carry):
            i = k * PER_CHUNK + j
            tile = lax.rem(ctx + STRIDE * i, CTX)
            pltpu.make_async_copy(halo_buf.at[i], halo_buf.at[i], halo_recv.at[i]).wait()
            group = (tile * TP + tp) * 2
            both = [circulant(long_rows[pl.ds(group + g, 1), :]) for g in range(2)]
            gain_row = jnp.broadcast_to(skip_ref[pl.ds(tile, 1), :], (CH, LANES))
            at = iota((CH, LANES), 1) == tp * CH + iota((CH, LANES), 0)
            gain = jnp.sum(jnp.where(at, gain_row, 0.0), axis=1, keepdims=True)
            blocks = [recv_buf[b, i, 0] for b in range(4)]
            earlier = [halo_buf[i]] + blocks[:3]
            masked = jnp.concatenate([earlier[b] * prev_mask[b] for b in range(4)], axis=0)
            weights = jnp.concatenate([both[0] * lower, both[1] * lower], axis=1)
            prev = pick(jnp.dot(masked, weights, preferred_element_type=F32))
            for b in range(4):
                weights = jnp.concatenate([both[0] * own_mask[b], both[1] * own_mask[b]], axis=1)
                total = pick(jnp.dot(blocks[b], weights, preferred_element_type=F32))
                total += prev[b * CH : (b + 1) * CH] * head_mask[b]
                total += gain * blocks[b].astype(F32)
                out_buf[i, :, b * LANES : (b + 1) * LANES] = (
                    recv_buf[b, i, 1].astype(F32) * total
                ).astype(BF16)
            place_at = pl.ds(pl.multiple_of(ctx * 512, 512), 512)

            @pl.when(i > 0)
            def _():
                pltpu.make_async_remote_copy(
                    out_buf.at[i],
                    out_ref.at[:, place_at],
                    two_send,
                    two_recv,
                    device_id=(tile, tp),
                    device_id_type=MESH,
                ).start()

            @pl.when(i == 0)
            def _():
                pltpu.make_async_copy(out_buf.at[0], out_ref.at[:, place_at], load_sem.at[0]).start()

            return carry

        lax.fori_loop(0, PER_CHUNK, one, 0)

    send_raw(0)
    for load in loads:
        load.wait()

    def step(n, carry):
        @pl.when(n + 1 < CHUNKS)
        def _():
            send_raw(n + 1)

        @pl.when(n < CHUNKS)
        def _():
            short_chunk(n)

        @pl.when((n >= 1) & (n <= CHUNKS))
        def _():
            forward_chunk(n - 1)

        @pl.when(n >= LAG)
        def _():
            long_chunk(n - LAG)

        return carry

    lax.fori_loop(0, CHUNKS + LAG, step, 0)

    pltpu.make_async_copy(raw_halo, raw_halo, raw_send).wait()
    pltpu.make_async_copy(send_buf.at[:, pl.ds(0, 3)], send_buf.at[:, pl.ds(0, 3)], one_send).wait()
    pltpu.make_async_copy(halo_buf, halo_buf, halo_send).wait()
    rest = out_buf.at[pl.ds(0, TILES - 1)]
    pltpu.make_async_copy(rest, rest, two_send).wait()
    pltpu.make_async_copy(out_buf.at[0], out_buf.at[0], load_sem.at[0]).wait()
    pltpu.make_async_copy(rest, rest, two_recv).wait()


def on_device(
    first_stream, second_stream, value_stream, short_filter, long_filter, skip_gain, lengths
):
    any_spec = pl.BlockSpec(memory_space=pl.ANY)
    vmem = pl.BlockSpec(memory_space=pltpu.VMEM)
    dma = pltpu.SemaphoreType.DMA
    return pl.pallas_call(
        kernel,
        out_shape=jax.ShapeDtypeStruct((CH, 32768), BF16),
        in_specs=[pl.BlockSpec(memory_space=pltpu.SMEM), any_spec, any_spec, any_spec, vmem, vmem, vmem],
        out_specs=any_spec,
        scratch_shapes=[
            pltpu.VMEM((3, ROWS, 8192), BF16),
            pltpu.VMEM((TILES, 3, HALO, LANES), BF16),
            pltpu.VMEM((3, HALO + ROWS, LANES), F32),
            pltpu.VMEM((TILES, 3, 8, LANES), F32),
            pltpu.VMEM((SHORT, ROWS, LANES), F32),
            pltpu.VMEM((512, LANES), F32),
            pltpu.VMEM((4, LANES, LANES), BF16),
            pltpu.VMEM((4, CH, LANES), BF16),
            pltpu.VMEM((4, CH, LANES), F32),
            pltpu.VMEM((TILES, TP, 2, CH, LANES), BF16),
            pltpu.VMEM((TP, TILES, 2, CH, LANES), BF16),
            pltpu.VMEM((TILES, CH, LANES), BF16),
            pltpu.VMEM((TILES, CH, 512), BF16),
            pltpu.VMEM((LANES, LANES), BF16),
            dma((3,)),
            dma,
            dma((CHUNKS,)),
            dma,
            dma((CHUNKS,)),
            dma((CHUNKS,)),
            dma,
            dma((TILES,)),
            dma,
            dma,
        ],
        compiler_params=pltpu.CompilerParams(
            collective_id=0, has_side_effects=True, vmem_limit_bytes=60 << 20
        ),
    )(lengths, first_stream, second_stream, value_stream, short_filter, long_filter, skip_gain.reshape(64, 128))


def solution(mesh):
    tokens = P(("ctx", "tp"), None)
    return jax.shard_map(
        on_device,
        mesh=mesh,
        in_specs=(tokens, tokens, tokens, P(), P(), P(), P()),
        out_specs=tokens,
        check_vma=False,
    )
```

profile of v0, /device:TPU:1, one launch (start us, length us, event | category | flops | bytes accessed | tf_op | source)
XLA Modules:
  0.0 102.9 jit_solution(4403481194106708742)
XLA Ops:
  0.0 99.9 %shard_map.73 = bf16[32,32768]{1,0:T(8,128)(2,1)} custom-call(s32[16]{0:T(128)} %lengths_ref.1, bf16[128,8192]{1,0:T(8,128)(2,1)} %first_hbm.1, bf16[128,8192]{1,0:T(8,128)(2,1)} %second_hbm.1, bf16[128,8192]{1,0:T(8,128)(2,1)} %value_hbm.1, bf16[3,7,512]{2,1,0:T(8,128)(2,1)} %short_ref.1, bf16[128,512]{1,0:T(8,128)(2,1)} %long_ref.1, f32[64,128]{1,0:T(8,128)} %bitcast.1), custom_call_target="tpu_custom_call" | custom-call | tf_op jit(solution)/shard_map/pallas_call | solution.py:304
  99.9 3.0 %copy.9 = bf16[32,32768]{1,0:T(8,128)(2,1)} copy(bf16[32,32768]{1,0:T(8,128)(2,1)} %shard_map.73) | data formatting | bytes 4194304
where the time goes:
time: 103 us
  Pallas kernels  99.9 us (97%)
  local copies, waits for them, and re-layouts  3.05 us (3%)
    pallas_call x1, Pallas kernels, on_device(): pl.pallas_call(kernel, out_shape=jax.ShapeDtypeStruct((CH, 32768), BF16),...  99.9 us
    unnamed x1, local copies, waits for them, and re-layouts  3.05 us

commit v1 on v0

--- a/solution.py
+++ b/solution.py
@@ -21,7 +21,11 @@
 HALO_LAG = 3
 PER_CHUNK = 4
 CHUNKS = TILES // PER_CHUNK
-LAG = 3
+LAG = 6
+AHEAD = 4
+FWD = 2
+UNROLL = 2
+REACH = (1, 2, 4, 8, 16)
 F32 = jnp.float32
 BF16 = jnp.bfloat16
 
@@ -53,10 +57,11 @@
 
 
 def kernel(
-    lengths_ref, first_hbm, second_hbm, value_hbm, short_ref, long_ref, skip_ref, out_ref,
+    lengths_ref, first_hbm, second_hbm, value_hbm, short_hbm, long_hbm, skip_hbm, out_ref,
+    short_ref, long_ref, skip_ref,
     streams, raw_halo, padded, taps, keep, long_rows, own_mask, prev_mask, head_mask,
-    send_buf, recv_buf, halo_buf, out_buf, ident,
-    load_sem, raw_send, raw_recv, one_send, one_recv, own_sem, halo_send, halo_recv, two_send, two_recv,
+    send_buf, recv_buf, halo_buf, out_buf, ident, early, partial,
+    load_sem, raw_send, raw_recv, one_send, one_recv, own_sem, halo_send, halo_recv, two_send, two_recv, met,
 ):
     ctx = lax.axis_index("ctx")
     tp = lax.axis_index("tp")
@@ -68,12 +73,6 @@
 
     barrier = pltpu.get_barrier_semaphore()
 
-    def greet(i, carry):
-        pl.semaphore_signal(
-            barrier, inc=1, device_id=(lax.rem(ctx + i, CTX), tp), device_id_type=MESH
-        )
-        return carry
-
     for d in range(1, TP):
         pl.semaphore_signal(
             barrier, inc=1, device_id=(ctx, lax.rem(tp + d, TP)), device_id_type=MESH
@@ -82,13 +81,24 @@
         pl.semaphore_signal(
             barrier, inc=1, device_id=(other // TP, lax.rem(other, TP)), device_id_type=MESH
         )
-    lax.fori_loop(1, CTX, greet, 0)
+    for d in (1, CTX - 1):
+        pl.semaphore_signal(
+            barrier, inc=1, device_id=(lax.rem(ctx + d, CTX), tp), device_id_type=MESH
+        )
 
     loads = [
         pltpu.make_async_copy(sources[s], streams.at[s], load_sem.at[s]) for s in range(3)
     ]
-    for load in loads:
+    small = [
+        pltpu.make_async_copy(src, dst, load_sem.at[3 + j])
+        for j, (src, dst) in enumerate(
+            ((short_hbm, short_ref), (long_hbm, long_ref), (skip_hbm, skip_ref))
+        )
+    ]
+    for load in small + loads:
         load.start()
+    for load in small:
+        load.wait()
 
     spread = (iota((LANES, 2048), 1) // 16 == iota((LANES, 2048), 0)).astype(BF16)
     for s in range(3):
@@ -120,7 +130,18 @@
         row_at = base + iota((CH, LANES), 1)
         head_mask[b] = jnp.where(starts_of(lengths_ref, row_at) <= base, 1.0, 0.0)
 
-    pl.semaphore_wait(barrier, CTX - 1 + TP - 1 + 2)
+    pl.semaphore_wait(barrier, 2 + TP - 1 + 2)
+
+    def reach(j):
+        for d in (REACH[j], CTX - REACH[j]):
+            pl.semaphore_signal(
+                met.at[j], inc=1, device_id=(lax.rem(ctx + d, CTX), tp), device_id_type=MESH
+            )
+
+    def met_all(j):
+        pl.semaphore_wait(met.at[j], 2)
+
+    reach(0)
 
     def send_raw(k):
         def one(j, carry):
@@ -143,27 +164,31 @@
         here = raw_halo.at[pl.ds(k * PER_CHUNK, PER_CHUNK)]
         pltpu.make_async_copy(here, here, raw_recv.at[k]).wait()
 
-        def one(j, carry):
-            i = k * PER_CHUNK + j
+        def one(i, u):
             tile = lax.rem(ctx + STRIDE * i, CTX)
             lanes = pl.ds(pl.multiple_of(tile * LANES, LANES), LANES)
             features = []
             for s in range(3):
-                padded[s, 0:HALO, :] = raw_halo[i, s].astype(F32)
-                padded[s, HALO:, :] = streams[s, :, lanes].astype(F32)
+                padded[u, s, 0:HALO, :] = raw_halo[i, s].astype(F32)
+                padded[u, s, HALO:, :] = streams[s, :, lanes].astype(F32)
             for s in range(3):
-                total = padded[s, HALO:, :] * taps[tile, s, 0:1, :]
+                total = padded[u, s, HALO:, :] * taps[tile, s, 0:1, :]
                 for t in range(1, SHORT):
-                    total += (padded[s, HALO - t : HALO - t + ROWS, :] * keep[t]) * taps[tile, s, t : t + 1, :]
+                    total += (padded[u, s, HALO - t : HALO - t + ROWS, :] * keep[t]) * taps[tile, s, t : t + 1, :]
                 features.append(total)
             mixed_in = (features[0] * features[2]).astype(BF16)
             gate = features[1].astype(BF16)
             unit = ident[...]
-            send_buf[i, :, 0] = nt_dot(unit, mixed_in).astype(BF16).reshape(TP, CH, LANES)
-            send_buf[i, :, 1] = nt_dot(unit, gate).astype(BF16).reshape(TP, CH, LANES)
+            turned = nt_dot(unit, jnp.concatenate([mixed_in, gate], axis=0)).astype(BF16)
+            send_buf[i, :, 0] = turned[:, :LANES].reshape(TP, CH, LANES)
+            send_buf[i, :, 1] = turned[:, LANES:].reshape(TP, CH, LANES)
+
+        def some(j, carry):
+            for u in range(UNROLL):
+                one(k * PER_CHUNK + j * UNROLL + u, u)
             return carry
 
-        lax.fori_loop(0, PER_CHUNK, one, 0)
+        lax.fori_loop(0, PER_CHUNK // UNROLL, some, 0)
         part = pl.ds(k * PER_CHUNK, PER_CHUNK)
         for d in range(1, TP):
             to = lax.rem(tp + d, TP)
@@ -217,70 +242,110 @@
             parts.append(wide[r * CH + 16 : (r + 1) * CH, LANES:])
         return jnp.concatenate(parts, axis=0)
 
-    def long_chunk(k):
-        def one(j, carry):
-            i = k * PER_CHUNK + j
-            tile = lax.rem(ctx + STRIDE * i, CTX)
-            pltpu.make_async_copy(halo_buf.at[i], halo_buf.at[i], halo_recv.at[i]).wait()
-            group = (tile * TP + tp) * 2
-            both = [circulant(long_rows[pl.ds(group + g, 1), :]) for g in range(2)]
-            gain_row = jnp.broadcast_to(skip_ref[pl.ds(tile, 1), :], (CH, LANES))
-            at = iota((CH, LANES), 1) == tp * CH + iota((CH, LANES), 0)
-            gain = jnp.sum(jnp.where(at, gain_row, 0.0), axis=1, keepdims=True)
-            blocks = [recv_buf[b, i, 0] for b in range(4)]
-            earlier = [halo_buf[i]] + blocks[:3]
-            masked = jnp.concatenate([earlier[b] * prev_mask[b] for b in range(4)], axis=0)
-            weights = jnp.concatenate([both[0] * lower, both[1] * lower], axis=1)
-            prev = pick(jnp.dot(masked, weights, preferred_element_type=F32))
-            for b in range(4):
-                weights = jnp.concatenate([both[0] * own_mask[b], both[1] * own_mask[b]], axis=1)
-                total = pick(jnp.dot(blocks[b], weights, preferred_element_type=F32))
-                total += prev[b * CH : (b + 1) * CH] * head_mask[b]
-                total += gain * blocks[b].astype(F32)
+    def ship(i, lo, width, sem):
+        tile = lax.rem(ctx + STRIDE * i, CTX)
+        to = pl.ds(pl.multiple_of(ctx * 512 + lo, LANES), width)
+        part = out_buf.at[i, :, pl.ds(lo, width)]
+
+        @pl.when(i > 0)
+        def _():
+            pltpu.make_async_remote_copy(
+                part,
+                out_ref.at[:, to],
+                two_send,
+                two_recv,
+                device_id=(tile, tp),
+                device_id_type=MESH,
+            ).start()
+
+        @pl.when(i == 0)
+        def _():
+            pltpu.make_async_copy(part, out_ref.at[:, to], load_sem.at[sem]).start()
+
+    def main_tile(i):
+        tile = lax.rem(ctx + STRIDE * i, CTX)
+        group = (tile * TP + tp) * 2
+        both = [circulant(long_rows[pl.ds(group + g, 1), :]) for g in range(2)]
+        gain_row = jnp.broadcast_to(skip_ref[pl.ds(tile, 1), :], (CH, LANES))
+        at = iota((CH, LANES), 1) == tp * CH + iota((CH, LANES), 0)
+        gain = jnp.sum(jnp.where(at, gain_row, 0.0), axis=1, keepdims=True)
+        blocks = [recv_buf[b, i, 0] for b in range(4)]
+        masked = jnp.concatenate([blocks[b - 1] * prev_mask[b] for b in range(1, 4)], axis=0)
+        weights = jnp.concatenate([both[0] * lower, both[1] * lower], axis=1)
+        early[i] = weights
+        prev = pick(jnp.dot(masked, weights, preferred_element_type=F32))
+        for b in range(4):
+            weights = jnp.concatenate([both[0] * own_mask[b], both[1] * own_mask[b]], axis=1)
+            total = pick(jnp.dot(blocks[b], weights, preferred_element_type=F32))
+            total += gain * blocks[b].astype(F32)
+            if b == 0:
+                partial[i] = total
+            else:
+                total += prev[(b - 1) * CH : b * CH] * head_mask[b]
                 out_buf[i, :, b * LANES : (b + 1) * LANES] = (
                     recv_buf[b, i, 1].astype(F32) * total
                 ).astype(BF16)
-            place_at = pl.ds(pl.multiple_of(ctx * 512, 512), 512)
-
-            @pl.when(i > 0)
-            def _():
-                pltpu.make_async_remote_copy(
-                    out_buf.at[i],
-                    out_ref.at[:, place_at],
-                    two_send,
-                    two_recv,
-                    device_id=(tile, tp),
-                    device_id_type=MESH,
-                ).start()
-
-            @pl.when(i == 0)
-            def _():
-                pltpu.make_async_copy(out_buf.at[0], out_ref.at[:, place_at], load_sem.at[0]).start()
-
+
+    def head_tile(i):
+        prev = pick(jnp.dot(halo_buf[i] * prev_mask[0], early[i], preferred_element_type=F32))
+        total = partial[i] + prev * head_mask[0]
+        out_buf[i, :, 0:LANES] = (recv_buf[0, i, 1].astype(F32) * total).astype(BF16)
+
+    def main_chunk(k):
+        def some(j, carry):
+            first = k * PER_CHUNK + j * UNROLL
+            for u in range(UNROLL):
+                main_tile(first + u)
+            for u in range(UNROLL):
+                ship(first + u, LANES, 3 * LANES, 0)
             return carry
 
-        lax.fori_loop(0, PER_CHUNK, one, 0)
-
-    send_raw(0)
+        lax.fori_loop(0, PER_CHUNK // UNROLL, some, 0)
+
+    def head_chunk(k):
+        def some(j, carry):
+            first = k * PER_CHUNK + j * UNROLL
+            for u in range(UNROLL):
+                here = halo_buf.at[first + u]
+                pltpu.make_async_copy(here, here, halo_recv.at[first + u]).wait()
+            for u in range(UNROLL):
+                head_tile(first + u)
+            for u in range(UNROLL):
+                ship(first + u, 0, LANES, 1)
+            return carry
+
+        lax.fori_loop(0, PER_CHUNK // UNROLL, some, 0)
+
+    for k in range(AHEAD):
+        send_raw(k)
     for load in loads:
         load.wait()
 
     def step(n, carry):
-        @pl.when(n + 1 < CHUNKS)
-        def _():
-            send_raw(n + 1)
+        @pl.when(n + AHEAD < CHUNKS)
+        def _():
+            send_raw(n + AHEAD)
 
         @pl.when(n < CHUNKS)
         def _():
             short_chunk(n)
 
-        @pl.when((n >= 1) & (n <= CHUNKS))
-        def _():
-            forward_chunk(n - 1)
+        for j in range(len(REACH)):
+
+            @pl.when(n == (j + 1) // 2)
+            def _():
+                met_all(j)
+                if j + 1 < len(REACH):
+                    reach(j + 1)
+
+        @pl.when((n >= FWD) & (n < CHUNKS + FWD))
+        def _():
+            forward_chunk(n - FWD)
+            main_chunk(n - FWD)
 
         @pl.when(n >= LAG)
         def _():
-            long_chunk(n - LAG)
+            head_chunk(n - LAG)
 
         return carry
 
@@ -291,7 +356,10 @@
     pltpu.make_async_copy(halo_buf, halo_buf, halo_send).wait()
     rest = out_buf.at[pl.ds(0, TILES - 1)]
     pltpu.make_async_copy(rest, rest, two_send).wait()
-    pltpu.make_async_copy(out_buf.at[0], out_buf.at[0], load_sem.at[0]).wait()
+    tail = out_buf.at[0, :, pl.ds(LANES, 3 * LANES)]
+    pltpu.make_async_copy(tail, tail, load_sem.at[0]).wait()
+    head = out_buf.at[0, :, pl.ds(0, LANES)]
+    pltpu.make_async_copy(head, head, load_sem.at[1]).wait()
     pltpu.make_async_copy(rest, rest, two_recv).wait()
 
 
@@ -299,17 +367,20 @@
     first_stream, second_stream, value_stream, short_filter, long_filter, skip_gain, lengths
 ):
     any_spec = pl.BlockSpec(memory_space=pl.ANY)
-    vmem = pl.BlockSpec(memory_space=pltpu.VMEM)
+    hbm = pl.BlockSpec(memory_space=pltpu.HBM)
     dma = pltpu.SemaphoreType.DMA
     return pl.pallas_call(
         kernel,
         out_shape=jax.ShapeDtypeStruct((CH, 32768), BF16),
-        in_specs=[pl.BlockSpec(memory_space=pltpu.SMEM), any_spec, any_spec, any_spec, vmem, vmem, vmem],
+        in_specs=[pl.BlockSpec(memory_space=pltpu.SMEM), hbm, hbm, hbm, hbm, hbm, hbm],
         out_specs=any_spec,
         scratch_shapes=[
+            pltpu.VMEM((3, SHORT, 512), BF16),
+            pltpu.VMEM((LANES, 512), BF16),
+            pltpu.VMEM((64, LANES), F32),
             pltpu.VMEM((3, ROWS, 8192), BF16),
             pltpu.VMEM((TILES, 3, HALO, LANES), BF16),
-            pltpu.VMEM((3, HALO + ROWS, LANES), F32),
+            pltpu.VMEM((UNROLL, 3, HALO + ROWS, LANES), F32),
             pltpu.VMEM((TILES, 3, 8, LANES), F32),
             pltpu.VMEM((SHORT, ROWS, LANES), F32),
             pltpu.VMEM((512, LANES), F32),
@@ -321,7 +392,9 @@
             pltpu.VMEM((TILES, CH, LANES), BF16),
             pltpu.VMEM((TILES, CH, 512), BF16),
             pltpu.VMEM((LANES, LANES), BF16),
-            dma((3,)),
+            pltpu.VMEM((TILES, LANES, 2 * LANES), BF16),
+            pltpu.VMEM((TILES, CH, LANES), F32),
+            dma((6,)),
             dma,
             dma((CHUNKS,)),
             dma,
@@ -331,11 +404,12 @@
             dma((TILES,)),
             dma,
             dma,
+            pltpu.SemaphoreType.REGULAR((len(REACH),)),
         ],
         compiler_params=pltpu.CompilerParams(
-            collective_id=0, has_side_effects=True, vmem_limit_bytes=60 << 20
+            collective_id=0, has_side_effects=True, vmem_limit_bytes=50 << 20
         ),
-    )(lengths, first_stream, second_stream, value_stream, short_filter, long_filter, skip_gain.reshape(64, 128))
+    )(*(pltpu.with_memory_space_constraint(x, pltpu.HBM) for x in (lengths, first_stream, second_stream, value_stream, short_filter, long_filter, skip_gain.reshape(64, 128))))
 
 
 def solution(mesh):

time: 103 us -> 83.5 us (0.81)
  Pallas kernels: 99.9 us -> 81.4 us
  local copies, waits for them, and re-layouts: 3.05 us -> 1.32 us
    pallas_call x1, Pallas kernels: 99.9 us -> 81.4 us  [on_device(): pl.pallas_call(kernel, out_shape=jax.ShapeDtypeStruct((CH, 32768), BF16),...]
    unnamed x1, local copies, waits for them, and re-layouts: 3.05 us -> 1.32 us
where the time goes in v1:
time: 83.5 us; the launch traced here: 82.8 us
  Pallas kernels  81.4 us (97%)
  local copies, waits for them, and re-layouts  1.32 us (2%)
    pallas_call x1, Pallas kernels, on_device(): pl.pallas_call(kernel, out_shape=jax.ShapeDtypeStruct((CH, 32768), BF16),...  81.4 us

profile of v1, /device:TPU:1, one launch (start us, length us, event | category | flops | bytes accessed | tf_op | source)
XLA Modules:
  0.0 82.8 jit_solution(11045294074930892767)
XLA Ops:
  0.0 81.4 %shard_map.73 = bf16[32,32768]{1,0:T(8,128)(2,1)S(1)} custom-call(s32[16]{0:T(128)} %lengths_ref.1, bf16[128,8192]{1,0:T(8,128)(2,1)} %first_hbm.1, bf16[128,8192]{1,0:T(8,128)(2,1)} %second_hbm.1, bf16[128,8192]{1,0:T(8,128)(2,1)} %value_hbm.1, bf16[3,7,512]{2,1,0:T(8,128)(2,1)} %short_hbm.1, bf16[128,512]{1,0:T(8,128)(2,1)} %long_hbm.1, f32[64,128]{1,0:T(8,128)} %bitcast.1), custom_call_target="tpu_custom_call" | custom-call | tf_op jit(solution)/shard_map/pallas_call | solution.py:372
  81.4 1.3 %copy.9 = bf16[32,32768]{1,0:T(8,128)(2,1)} copy(bf16[32,32768]{1,0:T(8,128)(2,1)S(1)} %shard_map.73) | data formatting | bytes 4194304

commit v2 on v1

--- a/solution.py
+++ b/solution.py
@@ -21,8 +21,8 @@
 HALO_LAG = 3
 PER_CHUNK = 4
 CHUNKS = TILES // PER_CHUNK
-LAG = 6
-AHEAD = 4
+LAG = 4
+AHEAD = 3
 FWD = 2
 UNROLL = 2
 REACH = (1, 2, 4, 8, 16)
@@ -59,7 +59,7 @@
 def kernel(
     lengths_ref, first_hbm, second_hbm, value_hbm, short_hbm, long_hbm, skip_hbm, out_ref,
     short_ref, long_ref, skip_ref,
-    streams, raw_halo, padded, taps, keep, long_rows, own_mask, prev_mask, head_mask,
+    streams, raw_out, raw_halo, padded, taps, keep, long_rows, own_mask, prev_mask, head_mask,
     send_buf, recv_buf, halo_buf, out_buf, ident, early, partial,
     load_sem, raw_send, raw_recv, one_send, one_recv, own_sem, halo_send, halo_recv, two_send, two_recv, met,
 ):
@@ -147,18 +147,23 @@
         def one(j, carry):
             i = k * PER_CHUNK + j
             tile = lax.rem(after_ctx + STRIDE * i, CTX)
+            lanes = pl.ds(pl.multiple_of(tile * LANES, LANES), LANES)
             for s in range(3):
-                pltpu.make_async_remote_copy(
-                    sources[s].at[pl.ds(ROWS - HALO, HALO), pl.ds(pl.multiple_of(tile * LANES, LANES), LANES)],
-                    raw_halo.at[i, s],
-                    raw_send,
-                    raw_recv.at[k],
-                    device_id=(after_ctx, after_tp),
-                    device_id_type=MESH,
-                ).start()
+                last = streams[s, ROWS - 16 : ROWS, lanes].astype(F32)
+                for h in range(3):
+                    raw_out[i, s, h] = last[10 + 2 * h : 12 + 2 * h].astype(BF16)
             return carry
 
         lax.fori_loop(0, PER_CHUNK, one, 0)
+        part = pl.ds(k * PER_CHUNK, PER_CHUNK)
+        pltpu.make_async_remote_copy(
+            raw_out.at[part],
+            raw_halo.at[part],
+            raw_send,
+            raw_recv.at[k],
+            device_id=(after_ctx, after_tp),
+            device_id_type=MESH,
+        ).start()
 
     def short_chunk(k):
         here = raw_halo.at[pl.ds(k * PER_CHUNK, PER_CHUNK)]
@@ -169,7 +174,8 @@
             lanes = pl.ds(pl.multiple_of(tile * LANES, LANES), LANES)
             features = []
             for s in range(3):
-                padded[u, s, 0:HALO, :] = raw_halo[i, s].astype(F32)
+                for h in range(3):
+                    padded[u, s, 2 + 2 * h : 4 + 2 * h, :] = raw_halo[i, s, h].astype(F32)
                 padded[u, s, HALO:, :] = streams[s, :, lanes].astype(F32)
             for s in range(3):
                 total = padded[u, s, HALO:, :] * taps[tile, s, 0:1, :]
@@ -316,10 +322,10 @@
 
         lax.fori_loop(0, PER_CHUNK // UNROLL, some, 0)
 
+    for load in loads:
+        load.wait()
     for k in range(AHEAD):
         send_raw(k)
-    for load in loads:
-        load.wait()
 
     def step(n, carry):
         @pl.when(n + AHEAD < CHUNKS)
@@ -379,7 +385,8 @@
             pltpu.VMEM((LANES, 512), BF16),
             pltpu.VMEM((64, LANES), F32),
             pltpu.VMEM((3, ROWS, 8192), BF16),
-            pltpu.VMEM((TILES, 3, HALO, LANES), BF16),
+            pltpu.VMEM((TILES, 3, 3, 2, LANES), BF16),
+            pltpu.VMEM((TILES, 3, 3, 2, LANES), BF16),
             pltpu.VMEM((UNROLL, 3, HALO + ROWS, LANES), F32),
             pltpu.VMEM((TILES, 3, 8, LANES), F32),
             pltpu.VMEM((SHORT, ROWS, LANES), F32),

time: 83.5 us -> 83.5 us (level)
  no operation moved by 1% of the time
where the time goes in v2:
time: 83.5 us; the launch traced here: 83.4 us
  Pallas kernels  82.1 us (98%)
  local copies, waits for them, and re-layouts  1.32 us (2%)
    pallas_call x1, Pallas kernels, on_device(): pl.pallas_call(kernel, out_shape=jax.ShapeDtypeStruct((CH, 32768), BF16),...  82.1 us

profile of v2, /device:TPU:1, one launch (start us, length us, event | category | flops | bytes accessed | tf_op | source)
XLA Modules:
  0.0 83.4 jit_solution(13426897992603114017)
XLA Ops:
  0.0 82.1 %shard_map.73 = bf16[32,32768]{1,0:T(8,128)(2,1)S(1)} custom-call(s32[16]{0:T(128)} %lengths_ref.1, bf16[128,8192]{1,0:T(8,128)(2,1)} %first_hbm.1, bf16[128,8192]{1,0:T(8,128)(2,1)} %second_hbm.1, bf16[128,8192]{1,0:T(8,128)(2,1)} %value_hbm.1, bf16[3,7,512]{2,1,0:T(8,128)(2,1)} %short_hbm.1, bf16[128,512]{1,0:T(8,128)(2,1)} %long_hbm.1, f32[64,128]{1,0:T(8,128)} %bitcast.1), custom_call_target="tpu_custom_call" | custom-call | tf_op jit(solution)/shard_map/pallas_call | solution.py:378
  82.1 1.3 %copy.9 = bf16[32,32768]{1,0:T(8,128)(2,1)} copy(bf16[32,32768]{1,0:T(8,128)(2,1)S(1)} %shard_map.73) | data formatting | bytes 4194304
